TPU v7x, 256 devices: a whole 4x4x8 slice. The times are simulated.
256 devices in a mesh: row: 16 (over y, x), col: 16 (over z, core).
Axes of the slice: x: 4, y: 4, z: 8, core: 2. Of those that a mesh axis runs over, the one named last changes fastest.
Arguments:
- hidden_in: bfloat16 [1024, 4096], P('col', 'row'), may hold values from -250 to 250
- norm_gain: bfloat16 [4096], P('row'), may hold values from 0.099609375 to 1.8984375
- w_qkv: bfloat16 [4096, 6144], P('row', 'col'), may hold values from -0.125 to 0.125
- w_out: bfloat16 [4096, 4096], P('row', 'col'), may hold values from -0.125 to 0.125
- cache_k: bfloat16 [16, 4096, 1024], P('col', 'row'), may hold values from -1300 to 1300
- value_cache: bfloat16 [16, 4096, 1024], P('col', 'row'), may hold values from -6 to 6
- cache_len: int32 [16], P('col'), may hold values from 1 to 4096, as said below
- parents: int32 [16, 64], P('col'), may hold values from -1 to 62, as said below
Outputs:
- update: bfloat16 [1024, 4096], P('col', 'row')
Inputs may be any that keep to these rules, and one draw needn't show every extreme that they name: Slots 0 to cache_len - 1 of a request's window are filled; some request fills all 4096 slots. `parents`: slot 0 of every request is the root with parent -1; every other slot's parent is an earlier slot of the same request; slot 63 has parent 64 - 2.
All inputs are finite; a program needn't handle non-finite values.
Results may differ from a plain program's by a relative error of at most 0.011.
The roundings to bfloat16 on the way count: a program that leaves them out, or rounds other values in their place, can miss the bound.
Values may be sent and summed in bfloat16 or wider, within the bound.
A program may use at most 128 MiB of HBM per device.

v0:
```python
import jax
import jax.numpy as jnp
from jax import lax
from jax.sharding import PartitionSpec as P

D = 4096
QUERY_HEADS = 32
KEY_VALUE_HEADS = 8
HEAD_SIZE = 128
masked_score = -1e30


def merged(value, axis, join):
    pieces = jax.tree.map(lambda part: lax.all_gather(part, axis), value)
    head = jax.tree.map(lambda part: part[0], pieces)
    tail = jax.tree.map(lambda part: part[1:], pieces)
    so_far, _ = lax.scan(lambda so_far, piece: (join(so_far, piece), None), head, tail)
    return so_far


def ancestors(parents):
    draft_tree = parents.shape[1]
    slot_ids = jnp.arange(draft_tree, dtype=jnp.int32)
    parent_links = (parents[:, :, None] == slot_ids[None, None, :]).astype(jnp.float32)
    reachable = parent_links + jnp.eye(draft_tree, dtype=jnp.float32)[None]
    for squaring in range(max(1, (draft_tree - 1).bit_length())):
        product = jnp.einsum("rij,rjk->rik", reachable, reachable, precision=lax.Precision.HIGHEST)
        reachable = (product > 0.5).astype(jnp.float32)
    return reachable > 0.5


def pair_merge(first, second):
    peak = jnp.maximum(first[0], second[0])
    first_scale = jnp.exp(first[0] - peak)
    second_scale = jnp.exp(second[0] - peak)
    totals = first[1] * first_scale + second[1] * second_scale
    blended = first[2] * first_scale[..., None] + second[2] * second_scale[..., None]
    return (peak, totals, blended)


def shards(hidden_in, norm_gain, w_qkv, w_out, cache_k, value_cache, cache_len, parents):
    rows_here = hidden_in.shape[0]
    request_list = cache_k.shape[0]
    token_positions = cache_k.shape[1]
    draft_tree = parents.shape[1]
    head_groups = QUERY_HEADS // KEY_VALUE_HEADS
    heads_dev = QUERY_HEADS // lax.axis_size("row")
    row_index = lax.axis_index("row")
    score_scale = HEAD_SIZE ** (-0.5)
    features = hidden_in.astype(jnp.float32)
    squares = lax.psum(jnp.sum(features * features, axis=1), "row")
    row_scale = lax.rsqrt(squares / D + 1e-05)
    normed = (features * row_scale[:, None] * norm_gain.astype(jnp.float32)[None, :]).astype(
        jnp.bfloat16
    )
    partial_value = jnp.dot(
        normed, lax.all_gather(w_qkv, "col", axis=1, tiled=True), preferred_element_type=jnp.float32
    )
    summed = lax.psum_scatter(partial_value, "row", scatter_dimension=1, tiled=True).astype(
        jnp.bfloat16
    )
    projected_output = lax.all_gather(summed, "row", axis=1, tiled=True)
    query_block = projected_output[:, : QUERY_HEADS * HEAD_SIZE].reshape(
        request_list, draft_tree, KEY_VALUE_HEADS, head_groups, HEAD_SIZE
    )
    new_key_block = projected_output[
        :, QUERY_HEADS * HEAD_SIZE : (QUERY_HEADS + KEY_VALUE_HEADS) * HEAD_SIZE
    ].reshape(request_list, draft_tree, KEY_VALUE_HEADS, HEAD_SIZE)
    new_value_block = projected_output[:, (QUERY_HEADS + KEY_VALUE_HEADS) * HEAD_SIZE :].reshape(
        request_list, draft_tree, KEY_VALUE_HEADS, HEAD_SIZE
    )
    first_slot = row_index * token_positions
    slot_ids = first_slot + jnp.arange(token_positions, dtype=jnp.int32)

    def cache_part(request_item):
        query_rows, cached_key_rows, cached_value_rows, length = request_item
        key_row_block = cached_key_rows.reshape(token_positions, KEY_VALUE_HEADS, HEAD_SIZE)
        value_row_block = cached_value_rows.reshape(token_positions, KEY_VALUE_HEADS, HEAD_SIZE)
        scores = (
            jnp.einsum(
                "tkgd,pkd->kgtp", query_rows, key_row_block, preferred_element_type=jnp.float32
            )
            * score_scale
        )
        visible = (slot_ids < length)[None, None, None, :]
        scores = jnp.where(visible, scores, masked_score)
        highest = jnp.max(scores, axis=-1)
        weights = jnp.where(visible, jnp.exp(scores - highest[..., None]), 0.0)
        totals = jnp.sum(weights, axis=-1)
        blended = jnp.einsum(
            "kgtp,pkd->kgtd",
            weights.astype(jnp.bfloat16),
            value_row_block,
            preferred_element_type=jnp.float32,
        )
        return (
            highest.reshape(QUERY_HEADS, draft_tree),
            totals.reshape(QUERY_HEADS, draft_tree),
            blended.reshape(QUERY_HEADS, draft_tree, HEAD_SIZE),
        )

    maxima, totals, blended = lax.map(cache_part, (query_block, cache_k, value_cache, cache_len))
    maxima, totals, blended = merged((maxima, totals, blended), "row", pair_merge)
    max_own = lax.dynamic_slice_in_dim(maxima, row_index * heads_dev, heads_dev, 1)
    total_own = lax.dynamic_slice_in_dim(totals, row_index * heads_dev, heads_dev, 1)
    blend_own = lax.dynamic_slice_in_dim(blended, row_index * heads_dev, heads_dev, 1)
    allowed = ancestors(parents)[:, None, :, :]
    query_heads = projected_output[:, : QUERY_HEADS * HEAD_SIZE].reshape(
        request_list, draft_tree, QUERY_HEADS, HEAD_SIZE
    )
    query_own = lax.dynamic_slice_in_dim(query_heads, row_index * heads_dev, heads_dev, 2)
    key_own = lax.dynamic_slice_in_dim(
        jnp.repeat(new_key_block, head_groups, axis=2), row_index * heads_dev, heads_dev, 2
    )
    value_own = lax.dynamic_slice_in_dim(
        jnp.repeat(new_value_block, head_groups, axis=2), row_index * heads_dev, heads_dev, 2
    )
    tree_scores = (
        jnp.einsum("rthd,rshd->rhts", query_own, key_own, preferred_element_type=jnp.float32)
        * score_scale
    )
    tree_scores = jnp.where(allowed, tree_scores, masked_score)
    tree_max = jnp.max(tree_scores, axis=-1)
    tree_weights = jnp.where(allowed, jnp.exp(tree_scores - tree_max[..., None]), 0.0)
    tree_total = jnp.sum(tree_weights, axis=-1)
    tree_blend = jnp.einsum(
        "rhts,rshd->rhtd",
        tree_weights.astype(jnp.bfloat16),
        value_own,
        preferred_element_type=jnp.float32,
    )
    joint_max = jnp.maximum(max_own, tree_max)
    cache_scale = jnp.exp(max_own - joint_max)
    tree_scale = jnp.exp(tree_max - joint_max)
    numerator = blend_own * cache_scale[..., None] + tree_blend * tree_scale[..., None]
    denominator = total_own * cache_scale + tree_total * tree_scale
    attended = (numerator / denominator[..., None]).astype(jnp.bfloat16)
    attended = attended.transpose(0, 2, 1, 3).reshape(rows_here, heads_dev * HEAD_SIZE)
    partial_out = jnp.dot(
        attended,
        lax.all_gather(w_out, "col", axis=1, tiled=True),
        preferred_element_type=jnp.float32,
    )
    return lax.psum_scatter(partial_out, "row", scatter_dimension=1, tiled=True).astype(
        jnp.bfloat16
    )


def solution(mesh):
    placed = (
        P("col", "row"),
        P("row"),
        P("row", "col"),
        P("row", "col"),
        P("col", "row", None),
        P("col", "row", None),
        P("col"),
        P("col", None),
    )
    return jax.shard_map(
        shards, mesh=mesh, in_specs=placed, out_specs=P("col", "row"), check_vma=False
    )
```

profile of v0, /device:TPU:2, one launch (start us, length us, event | category | flops | bytes accessed | tf_op | source)
XLA Modules:
  0.0 420.8 jit_solution(8517399735573453257)
XLA Ops:
  8.8 37.7 %psum.7 = f32[64]{0:T(128)S(1)} all-reduce(f32[64]{0:T(128)S(1)} %fusion.29), channel_id=1, replica_groups=mesh['row'=16,'col'=16] {'row'}, use_global_device_ids=true, to_apply=%region_1.0 | all-reduce | flops 64 | bytes 512 | tf_op jit(solution)/shard_map/psum | solution.py:51
  46.5 6.5 %all-gather.4.cloned.1.call-done = bf16[256,6144]{1,0:T(8,128)(2,1)} async-done(((bf16[256,384]{1,0:T(8,128)(2,1)}), bf16[256,6144]{1,0:T(8,128)(2,1)}) %all-gather.4.cloned.1.call-update) | async-done | bytes 3145744 | tf_op jit(solution)/shard_map/all_gather | solution.py:57
  53.0 3.8 fusion.35
  59.3 75.1 %reduce-scatter.3.cloned.1.call-done = f32[64,384]{1,0:T(8,128)} async-done(((f32[64,6144]{1,0:T(8,128)}), f32[64,384]{1,0:T(8,128)}) %reduce-scatter.3.cloned.1.call-update) | async-done | bytes 98320 | tf_op jit(solution)/shard_map/reduce_scatter | solution.py:59
  135.3 22.6 %all_gather.28 = bf16[64,6144]{1,0:T(8,128)(2,1)S(1)} all-gather(bf16[64,384]{1,0:T(8,128)(2,1)S(1)} %convert_element_type.85), channel_id=1, replica_groups=mesh['row'=16,'col'=16] {'row'}, dimensions={1}, use_global_device_ids=true | all-gather | bytes 835584 | tf_op jit(solution)/shard_map/all_gather | solution.py:62
  158.1 1.2 squeeze.36
  159.3 1.9 bitcast_reduce_fusion
  161.2 1.6 fusion.17
  165.5 24.1 %all_gather.32 = f32[16,1,32,64]{3,2,1,0:T(8,128)S(1)} all-gather(f32[1,1,32,64]{3,2,1,0:T(8,128)S(1)} %bitcast.147), channel_id=1, replica_groups=mesh['row'=16,'col'=16] {'row'}, dimensions={0}, use_global_device_ids=true | all-gather | bytes 139264 | tf_op jit(solution)/shard_map/all_gather | solution.py:14
  189.6 22.0 %all_gather.30 = f32[16,1,32,64]{3,2,1,0:T(8,128)S(1)} all-gather(f32[1,1,32,64]{3,2,1,0:T(8,128)S(1)} %bitcast.146), channel_id=1, replica_groups=mesh['row'=16,'col'=16] {'row'}, dimensions={0}, use_global_device_ids=true | all-gather | bytes 139264 | tf_op jit(solution)/shard_map/all_gather | solution.py:14
  212.2 68.4 %all-gather.6.cloned.1.call-done = f32[16,1,32,64,128]{4,3,2,1,0:T(8,128)} async-done(((f32[1,1,32,64,128]{4,3,2,1,0:T(8,128)}), f32[16,1,32,64,128]{4,3,2,1,0:T(8,128)}) %all-gather.6.cloned.1.call-update) | async-done | bytes 16777232 | tf_op jit(solution)/shard_map/all_gather | solution.py:14
  280.6 1.3 slice_bitcast_fusion
  281.9 14.5 %slice.43 = f32[15,1,32,64,128]{4,3,2,1,0:T(8,128)} slice(f32[16,1,32,64,128]{4,3,2,1,0:T(8,128)} %all-gather.6.cloned.1.call-done), slice={[1:16], [0:1], [0:32], [0:64], [0:128]} | slice | bytes 31457280 | tf_op jit(solution)/shard_map/slice | solution.py:16
  296.5 34.1 %while.2 = (s32[]{:T(128)}, f32[1,32,64]{2,1,0:T(8,128)S(1)}, f32[1,32,64]{2,1,0:T(8,128)S(1)}, f32[1,32,64,128]{3,2,1,0:T(8,128)S(1)}, f32[15,1,32,64]{3,2,1,0:...) while((s32[]{:T(128)}, f32[1,32,64]{2,1,0:T(8,128)S(1)}, ...), condition=%wide.region_6.7_spmd, body=%wide.region_5.6_spmd.sunk | while | flops 800770 | bytes 3268713 | solution.py:17
  296.5 2.2 fusion.83
  298.8 2.2 fusion.83
  301.1 2.2 fusion.83
  303.4 2.2 fusion.83
  305.6 2.2 fusion.83
  307.9 2.2 fusion.83
  310.2 2.2 fusion.83
  312.5 2.2 fusion.83
  314.7 2.2 fusion.83
  317.0 2.2 fusion.83
  319.3 2.2 fusion.83
  321.6 2.2 fusion.83
  323.8 2.2 fusion.83
  326.1 2.2 fusion.83
  328.4 2.2 fusion.83
  331.0 3.0 fusion.38
  334.1 78.7 %reduce-scatter.5.cloned.1.call-done = f32[64,256]{1,0:T(8,128)} async-done(((f32[64,4096]{1,0:T(8,128)}), f32[64,256]{1,0:T(8,128)}) %reduce-scatter.5.cloned.1.call-update) | async-done | bytes 65552 | tf_op jit(solution)/shard_map/reduce_scatter | solution.py:144
  412.8 1.5 convert_element_type.92
  (96 shorter events, 9.4 us)
Async XLA Ops:
  6.5 46.5 %all-gather.4.cloned.1.call-start = ((), (), s32[]{:S(2)}) async-start(), calls=%async_computation.2 | async-start | bytes 3342336 | tf_op jit(solution)/shard_map/all_gather | solution.py:57
  7.3 127.2 %reduce-scatter.3.cloned.1.call-start = ((), (), s32[]{:S(2)}) async-start(), calls=%async_computation.3 | async-start | bytes 1671168 | tf_op jit(solution)/shard_map/reduce_scatter | solution.py:59
  46.5 11.0 %copy-start = (bf16[1,256,1024]{2,1,0:T(8,128)(2,1)S(1)}, bf16[1,256,1024]{2,1,0:T(8,128)(2,1)}, u32[]{:S(2)}) copy-start(bf16[1,256,1024]{2,1,0:T(8,128)(2,1)} %param.14) | copy-start | bytes 1572868
  56.8 1.7 copy-start.1
  56.8 223.8 %all-gather.6.cloned.1.call-start = ((), (), s32[]{:S(2)}) async-start(), calls=%async_computation.4 | async-start | bytes 17825792 | tf_op jit(solution)/shard_map/all_gather | solution.py:14
  159.3 1.9 copy-start.2
  161.2 2.3 copy-start.3
  162.8 168.2 %all-gather.8.cloned.1.call-start = ((), (), s32[]{:S(2)}) async-start(), calls=%async_computation.5 | async-start | bytes 2228224 | tf_op jit(solution)/shard_map/all_gather | solution.py:141
  163.4 249.4 %reduce-scatter.5.cloned.1.call-start = ((), (), s32[]{:S(2)}) async-start(), calls=%async_computation.6 | async-start | bytes 1114112 | tf_op jit(solution)/shard_map/reduce_scatter | solution.py:144
Sparse Core Ops, SparseCore 0:
  9.1 43.8 all-gather.3
  56.9 77.4 reduce-scatter.2
  162.9 117.6 all-gather.5
  282.2 40.3 all-gather.7
  334.2 78.5 reduce-scatter.4
where the time goes:
time: 422 us; the launch traced here: 421 us
  waiting for transfers between devices  230 us (55%)
  blocking collectives  106 us (25%)
  other arithmetic  38.4 us (9%)
  local copies, waits for them, and re-layouts  19.6 us (5%)
  between operations  14 us (3%)
  matrix products  11.5 us (3%)
    reduce_scatter x1, waiting for transfers between devices, shards(): lax.psum_scatter(partial_out, 'row', scatter_dimension=1, tiled=True)  78.7 us
    reduce_scatter x1, waiting for transfers between devices, shards(): lax.psum_scatter(partial_value, 'row', scatter_dimension=1, tiled=True)  75.1 us
    all_gather x1, waiting for transfers between devices, merged(): pieces = jax.tree.map(lambda part: lax.all_gather(part, axis), value)  68.4 us
    all_gather x2, blocking collectives, merged(): pieces = jax.tree.map(lambda part: lax.all_gather(part, axis), value)  46.1 us
    psum x1, blocking collectives, shards(): squares = lax.psum(jnp.sum(features * features, axis=1), 'row')  37.7 us
    add x15, other arithmetic, pair_merge(): first[2] * first_scale[..., None] + second[2] * second_scale[..., None]  32.9 us
    all_gather x1, blocking collectives, shards(): projected_output = lax.all_gather(summed, 'row', axis=1, tiled=True)  22.6 us
    slice x3, local copies, waits for them, and re-layouts, merged(): tail = jax.tree.map(lambda part: part[1:], pieces)  14.6 us
  transfers between devices with their start and end apart: 5, of which 4 were waited for; matrix products, arithmetic and copies ran while one was open for 13% of the time, Pallas kernels for 0%

commit v1 on v0

--- a/solution.py
+++ b/solution.py
@@ -48,7 +48,7 @@
     row_index = lax.axis_index("row")
     score_scale = HEAD_SIZE ** (-0.5)
     features = hidden_in.astype(jnp.float32)
-    squares = lax.psum(jnp.sum(features * features, axis=1), "row")
+    squares = jnp.sum(lax.all_gather(jnp.sum(features * features, axis=1), "row"), axis=0)
     row_scale = lax.rsqrt(squares / D + 1e-05)
     normed = (features * row_scale[:, None] * norm_gain.astype(jnp.float32)[None, :]).astype(
         jnp.bfloat16

time: 422 us -> 422 us (level)
    psum x1 -> x0, blocking collectives: 37.7 us -> none  [shards(): squares = lax.psum(jnp.sum(features * features, axis=1), 'row')]
    unnamed x0 -> x1, blocking collectives: none -> 37.7 us
  transfers between devices with their start and end apart: 5 -> 5, of which waited for: 4 -> 4; matrix products, arithmetic and copies ran while one was open for 13% -> 14% of each run, Pallas kernels for 0% -> 0%
where the time goes in v1:
time: 422 us; the launch traced here: 421 us
  waiting for transfers between devices  228 us (54%)
  blocking collectives  106 us (25%)
  other arithmetic  38.5 us (9%)
  local copies, waits for them, and re-layouts  21.2 us (5%)
  between operations  14.7 us (3%)
  matrix products  11.5 us (3%)
    reduce_scatter x1, waiting for transfers between devices, shards(): lax.psum_scatter(partial_out, 'row', scatter_dimension=1, tiled=True)  78.7 us
    reduce_scatter x1, waiting for transfers between devices, shards(): lax.psum_scatter(partial_value, 'row', scatter_dimension=1, tiled=True)  75.2 us
    all_gather x1, waiting for transfers between devices, merged(): pieces = jax.tree.map(lambda part: lax.all_gather(part, axis), value)  68.4 us
    all_gather x2, blocking collectives, merged(): pieces = jax.tree.map(lambda part: lax.all_gather(part, axis), value)  46.1 us
    unnamed x1, blocking collectives  37.7 us
    add x15, other arithmetic, pair_merge(): first[2] * first_scale[..., None] + second[2] * second_scale[..., None]  32.9 us
    all_gather x1, blocking collectives, shards(): projected_output = lax.all_gather(summed, 'row', axis=1, tiled=True)  22.6 us
    slice x3, local copies, waits for them, and re-layouts, merged(): tail = jax.tree.map(lambda part: part[1:], pieces)  14.6 us
  transfers between devices with their start and end apart: 5, of which 4 were waited for; matrix products, arithmetic and copies ran while one was open for 14% of the time, Pallas kernels for 0%

profile of v1, /device:TPU:2, one launch (start us, length us, event | category | flops | bytes accessed | tf_op | source)
XLA Modules:
  0.0 420.9 jit_solution(17388394330689839780)
XLA Ops:
  8.0 1.3 dynamic-slice.8
  11.0 37.7 %all-reduce = f32[1024]{0:T(1024)S(1)} all-reduce(f32[1024]{0:T(1024)S(1)} %dynamic-update-slice), channel_id=2, replica_groups=mesh['row'=16,'col'=16] {'row'}, use_global_device_ids=true, to_apply=%add | all-reduce | flops 1024 | bytes 8192
  48.8 4.2 all-gather.5.cloned.1.call-done
  53.0 3.8 fusion.35
  59.3 75.2 %reduce-scatter.3.cloned.1.call-done = f32[64,384]{1,0:T(8,128)} async-done(((f32[64,6144]{1,0:T(8,128)}), f32[64,384]{1,0:T(8,128)}) %reduce-scatter.3.cloned.1.call-update) | async-done | bytes 98320 | tf_op jit(solution)/shard_map/reduce_scatter | solution.py:59
  135.4 22.6 %all_gather.36 = bf16[64,6144]{1,0:T(8,128)(2,1)S(1)} all-gather(bf16[64,384]{1,0:T(8,128)(2,1)S(1)} %convert_element_type.85), channel_id=1, replica_groups=mesh['row'=16,'col'=16] {'row'}, dimensions={1}, use_global_device_ids=true | all-gather | bytes 835584 | tf_op jit(solution)/shard_map/all_gather | solution.py:62
  159.4 1.9 bitcast_reduce_fusion
  161.2 1.6 fusion.17
  165.6 24.1 %all_gather.40 = f32[16,1,32,64]{3,2,1,0:T(8,128)S(1)} all-gather(f32[1,1,32,64]{3,2,1,0:T(8,128)S(1)} %bitcast.148), channel_id=1, replica_groups=mesh['row'=16,'col'=16] {'row'}, dimensions={0}, use_global_device_ids=true | all-gather | bytes 139264 | tf_op jit(solution)/shard_map/all_gather | solution.py:14
  189.7 22.0 %all_gather.38 = f32[16,1,32,64]{3,2,1,0:T(8,128)S(1)} all-gather(f32[1,1,32,64]{3,2,1,0:T(8,128)S(1)} %bitcast.147), channel_id=1, replica_groups=mesh['row'=16,'col'=16] {'row'}, dimensions={0}, use_global_device_ids=true | all-gather | bytes 139264 | tf_op jit(solution)/shard_map/all_gather | solution.py:14
  212.3 68.4 %all-gather.7.cloned.1.call-done = f32[16,1,32,64,128]{4,3,2,1,0:T(8,128)} async-done(((f32[1,1,32,64,128]{4,3,2,1,0:T(8,128)}), f32[16,1,32,64,128]{4,3,2,1,0:T(8,128)}) %all-gather.7.cloned.1.call-update) | async-done | bytes 16777232 | tf_op jit(solution)/shard_map/all_gather | solution.py:14
  280.7 1.3 slice_bitcast_fusion
  282.0 14.5 %slice.43 = f32[15,1,32,64,128]{4,3,2,1,0:T(8,128)} slice(f32[16,1,32,64,128]{4,3,2,1,0:T(8,128)} %all-gather.7.cloned.1.call-done), slice={[1:16], [0:1], [0:32], [0:64], [0:128]} | slice | bytes 31457280 | tf_op jit(solution)/shard_map/slice | solution.py:16
  296.6 34.1 %while.2 = (s32[]{:T(128)}, f32[1,32,64]{2,1,0:T(8,128)S(1)}, f32[1,32,64]{2,1,0:T(8,128)S(1)}, f32[1,32,64,128]{3,2,1,0:T(8,128)S(1)}, f32[15,1,32,64]{3,2,1,0:...) while((s32[]{:T(128)}, f32[1,32,64]{2,1,0:T(8,128)S(1)}, ...), condition=%wide.region_6.7_spmd, body=%wide.region_5.6_spmd.sunk | while | flops 800770 | bytes 3268713 | solution.py:17
  296.6 2.2 fusion.83
  298.9 2.2 fusion.83
  301.2 2.2 fusion.83
  303.5 2.2 fusion.83
  305.8 2.2 fusion.83
  308.0 2.2 fusion.83
  310.3 2.2 fusion.83
  312.6 2.2 fusion.83
  314.8 2.2 fusion.83
  317.1 2.2 fusion.83
  319.4 2.2 fusion.83
  321.7 2.2 fusion.83
  323.9 2.2 fusion.83
  326.2 2.2 fusion.83
  328.5 2.2 fusion.83
  331.1 3.0 fusion.38
  334.2 78.7 %reduce-scatter.5.cloned.1.call-done = f32[64,256]{1,0:T(8,128)} async-done(((f32[64,4096]{1,0:T(8,128)}), f32[64,256]{1,0:T(8,128)}) %reduce-scatter.5.cloned.1.call-update) | async-done | bytes 65552 | tf_op jit(solution)/shard_map/reduce_scatter | solution.py:144
  412.9 1.5 convert_element_type.92
  (101 shorter events, 10.9 us)
Async XLA Ops:
  6.5 46.5 %all-gather.5.cloned.1.call-start = ((), (), s32[]{:S(2)}) async-start(), calls=%async_computation.2 | async-start | bytes 3342336 | tf_op jit(solution)/shard_map/all_gather | solution.py:57
  7.3 127.3 %reduce-scatter.3.cloned.1.call-start = ((), (), s32[]{:S(2)}) async-start(), calls=%async_computation.3 | async-start | bytes 1671168 | tf_op jit(solution)/shard_map/reduce_scatter | solution.py:59
  48.8 8.7 %copy-start = (bf16[1,256,1024]{2,1,0:T(8,128)(2,1)S(1)}, bf16[1,256,1024]{2,1,0:T(8,128)(2,1)}, u32[]{:S(2)}) copy-start(bf16[1,256,1024]{2,1,0:T(8,128)(2,1)} %param.14) | copy-start | bytes 1572868
  56.8 1.7 copy-start.1
  56.8 223.9 %all-gather.7.cloned.1.call-start = ((), (), s32[]{:S(2)}) async-start(), calls=%async_computation.4 | async-start | bytes 17825792 | tf_op jit(solution)/shard_map/all_gather | solution.py:14
  159.4 1.9 copy-start.2
  161.2 2.3 copy-start.3
  162.9 168.2 %all-gather.9.cloned.1.call-start = ((), (), s32[]{:S(2)}) async-start(), calls=%async_computation.5 | async-start | bytes 2228224 | tf_op jit(solution)/shard_map/all_gather | solution.py:141
  163.5 249.4 %reduce-scatter.5.cloned.1.call-start = ((), (), s32[]{:S(2)}) async-start(), calls=%async_computation.6 | async-start | bytes 1114112 | tf_op jit(solution)/shard_map/reduce_scatter | solution.py:144
Sparse Core Ops, SparseCore 0:
  9.1 43.8 all-gather.4
  56.9 77.5 reduce-scatter.2
  163.0 117.6 all-gather.6
  282.3 40.3 all-gather.8
  334.3 78.5 reduce-scatter.4
